TPU v7x, 32 devices: a whole 2x2x4 slice. The times are simulated.
32 devices in a mesh: swath: 2 (over x), rng: 16 (over z, y, core).
Axes of the slice: x: 2, y: 2, z: 4, core: 2. Of those that a mesh axis runs over, the one named last changes fastest.
Arguments:
- echoes: float32 [2, 512, 32768], P(None, ('swath', 'rng')), parts along dimension 1, may hold values from -6 to 6
- doppler_filter: float32 [2, 32768], replicated, may hold values from -5 to 5
- migration_shift: int32 [32768], replicated, may hold values from 0 to 9, as said below
- kernel_index: int32 [32768], replicated, may hold values from 0 to 15
- kernel_taps: float32 [16, 16], replicated, may hold values from -1.5 to 1.5
Outputs:
- image: float32 [2, 512, 32768], P(None, ('swath', 'rng')), parts along dimension 1
There are 2 independent parts, one for each index of `swath`. A program takes and returns all parts, laid end to end along the dimension named above; an argument that names none is the same for every part. Nothing has to cross between parts.
Inputs may be any that keep to these rules, and one draw needn't show every extreme that they name: `migration_shift`: both 0 and 9 occur.
All inputs are finite; a program needn't handle non-finite values.
Results may differ from a plain program's by a relative error of at most 0.0041.
Values may be sent and summed in bfloat16 or wider, within the bound.
A program may use at most 64 MiB of HBM per device.

v0:
```python
import functools
import math

import jax
import jax.numpy as jnp
import numpy as np
from jax import lax
from jax.experimental import pallas as pl
from jax.experimental.pallas import tpu as pltpu
from jax.sharding import PartitionSpec as P

F2 = 256
SMAX = 9
GROUP = 8
CHUNK = 16

f32 = jnp.float32
bf16 = jnp.bfloat16


def dft(length):
    numbers = np.arange(length)
    angles = (numbers[:, None] * numbers[None, :] % length) * (2.0 * math.pi / length)
    return np.cos(angles), np.sin(angles)


def split(table):
    table = table.astype(np.float32)
    high = table.astype(bf16)
    return high, (table - high.astype(np.float32)).astype(bf16)


def twiddles(outer, inner):
    angles = (np.arange(outer)[:, None] * np.arange(inner)[None, :]) * (
        2.0 * math.pi / (outer * inner)
    )
    return np.stack([np.cos(angles), np.sin(angles)]).astype(np.float32)


def dot(a, b):
    return jnp.dot(a, b, preferred_element_type=f32)


def halves(value):
    high = value.astype(bf16)
    return high, (value - high.astype(f32)).astype(bf16)


def forward_kernel(outer, inner, x_ref, w1h_ref, w1l_ref, w2h_ref, w2l_ref, t_ref, h_ref, o_ref, rh_ref, rl_ref):
    lanes = 128
    parts = inner // lanes
    stride = GROUP * parts
    w1h = w1h_ref[...]
    w1l = w1l_ref[...]
    for r in range(GROUP):
        columns = []
        for c in range(2):
            columns.append(
                jnp.concatenate(
                    [
                        x_ref[c, 0, pl.ds(h * GROUP + r, outer, stride=stride), :]
                        for h in range(parts)
                    ],
                    axis=1,
                )
            )
        xh, xl = halves(jnp.concatenate(columns, axis=0))
        s = dot(w1h, xh) + dot(w1h, xl) + dot(w1l, xh)
        re, im = s[:outer], s[outer:]
        tc, ts = t_ref[0], t_ref[1]
        rows = pl.ds(r * outer, outer)
        a, b = halves(re * tc + im * ts)
        rh_ref[rows, :inner] = a
        rl_ref[rows, :inner] = b
        a, b = halves(im * tc - re * ts)
        rh_ref[rows, inner:] = a
        rl_ref[rows, inner:] = b
    per = 2
    for g in range(GROUP // per):
        rows = pl.ds(g * per * outer, per * outer)
        rh = rh_ref[rows, :]
        z = dot(rh, w2h_ref[...]) + dot(rh, w2l_ref[...]) + dot(rl_ref[rows, :], w2h_ref[...])
        for j in range(per):
            re = z[j * outer : (j + 1) * outer, :inner]
            im = z[j * outer : (j + 1) * outer, inner:]
            hr, hi = h_ref[0], h_ref[1]
            o_ref[0, 0, g * per + j] = (re * hr + im * hi).astype(bf16)
            o_ref[0, 1, g * per + j] = (im * hr - re * hi).astype(bf16)


def inverse_kernel(outer, inner, rows, taps, chunks, own_ref, prev_ref, next_ref, s_ref, k_ref, tab_ref, t_ref, v2_ref, v1_ref, o_ref, m_ref, y_ref):
    lanes = 128
    parts = inner // lanes
    stride = GROUP * parts
    step = pl.program_id(0)
    low = taps // 2 - 1

    @pl.when(step < chunks)
    def _():
        for sub in range(CHUNK // 8):
            for part in range(parts):
                a = slice(sub * 8, sub * 8 + 8)
                b = slice(part * lanes, part * lanes + lanes)
                offset = SMAX - s_ref[a, b]
                which = k_ref[a, b]
                bits = [(offset & bit) != 0 for bit in (8, 4, 2, 1)]
                weights = [
                    jnp.take_along_axis(tab_ref[k], which, axis=1, mode="promise_in_bounds")
                    for k in range(taps)
                ]
                for c in range(2):
                    line = [prev_ref[g, c, i, a, b] for g in range(rows // GROUP) for i in range(GROUP)]
                    line += [own_ref[g, c, i, a, b] for g in range(rows // GROUP) for i in range(GROUP)]
                    line += [next_ref[0, c, i, a, b] for i in range(GROUP)]
                    line = [v.astype(f32) for v in line]
                    need = rows + taps - 1
                    for n, bit in enumerate((8, 4, 2, 1)):
                        keep = need + (bit - 1)
                        line = [
                            jnp.where(bits[n], line[j + bit], line[j]) if j + bit < len(line) else line[j]
                            for j in range(keep)
                        ]
                    for i in range(rows):
                        total = weights[0] * line[i + taps - 1]
                        for k in range(1, taps):
                            total = total + weights[k] * line[i + taps - 1 - k]
                        m_ref[i, a, c * inner + part * lanes : c * inner + part * lanes + lanes] = total
        flat = m_ref[...].reshape(rows * CHUNK, 2 * inner).astype(bf16)
        z = dot(flat, v2_ref[...]).reshape(rows, CHUNK, 2 * inner)
        re, im = z[:, :, :inner], z[:, :, inner:]
        tc, ts = t_ref[0][None], t_ref[1][None]
        first = pl.multiple_of(step * CHUNK, CHUNK)
        y_ref[:, 0, pl.ds(first, CHUNK), :] = (re * tc - im * ts).astype(bf16)
        y_ref[:, 1, pl.ds(first, CHUNK), :] = (re * ts + im * tc).astype(bf16)

    @pl.when(step >= chunks)
    def _():
        base = (step - chunks) * GROUP
        scale = 1.0 / math.sqrt(outer * inner)
        for r in range(GROUP):
            z = dot(v1_ref[...], y_ref[base + r].reshape(2 * outer, inner)) * scale
            for c in range(2):
                for h in range(parts):
                    o_ref[c, 0, pl.ds(h * GROUP + r, outer, stride=stride), :] = z[
                        c * outer : (c + 1) * outer, h * lanes : (h + 1) * lanes
                    ]


def per_device(echoes, doppler_filter, migration_shift, kernel_index, kernel_taps):
    rows = echoes.shape[1]
    pulses = echoes.shape[2]
    inner = F2
    outer = pulses // inner
    taps = kernel_taps.shape[1]
    groups = rows // GROUP
    tiles = pulses // 128
    count = lax.axis_size("rng")
    whole = lambda *shape: pl.BlockSpec(shape, lambda i: (0,) * len(shape))

    def order(table):
        return jnp.swapaxes(table.reshape(table.shape[:-1] + (inner, outer)), -1, -2)

    oc, osn = dft(outer)
    ic, isn = dft(inner)
    w1h, w1l = split(np.block([[oc, osn], [-osn, oc]]))
    w2h, w2l = split(np.block([[ic, -isn], [isn, ic]]))
    v2 = split(np.block([[ic, isn], [-isn, ic]]))[0]
    v1 = split(np.block([[oc, -osn], [osn, oc]]))[0]
    twist = twiddles(outer, inner)
    response = order(doppler_filter * (1.0 / math.sqrt(pulses)))
    signal = (
        echoes.reshape(2, groups, GROUP, tiles, 128)
        .transpose(0, 1, 3, 2, 4)
        .reshape(2, groups, tiles * GROUP, 128)
    )
    filtered = pl.pallas_call(
        functools.partial(forward_kernel, outer, inner),
        grid=(groups,),
        in_specs=[
            pl.BlockSpec((2, 1, tiles * GROUP, 128), lambda i: (0, i, 0, 0)),
            whole(*w1h.shape),
            whole(*w1h.shape),
            whole(*w2h.shape),
            whole(*w2h.shape),
            whole(*twist.shape),
            whole(*twist.shape),
        ],
        out_specs=pl.BlockSpec((1, 2, GROUP, outer, inner), lambda i: (i, 0, 0, 0, 0)),
        out_shape=jax.ShapeDtypeStruct((groups, 2, GROUP, outer, inner), bf16),
        scratch_shapes=[pltpu.VMEM((GROUP * outer, 2 * inner), bf16)] * 2,
        name="forward",
    )(signal, jnp.asarray(w1h), jnp.asarray(w1l), jnp.asarray(w2h), jnp.asarray(w2l), jnp.asarray(twist), response)
    before = lax.ppermute(filtered, "rng", [(i, i + 1) for i in range(count - 1)])
    after = lax.ppermute(filtered[:1], "rng", [(i + 1, i) for i in range(count - 1)])
    table = jnp.broadcast_to(
        jnp.tile(kernel_taps.T, (1, 128 // kernel_taps.shape[0]))[:, None, :], (taps, 8, 128)
    )
    chunks = outer // CHUNK
    last = chunks - 1
    at = lambda i: jnp.minimum(i, last)
    image = pl.pallas_call(
        functools.partial(inverse_kernel, outer, inner, rows, taps, chunks),
        grid=(chunks + groups,),
        in_specs=[
            pl.BlockSpec((groups, 2, GROUP, CHUNK, inner), lambda i: (0, 0, 0, at(i), 0)),
            pl.BlockSpec((groups, 2, GROUP, CHUNK, inner), lambda i: (0, 0, 0, at(i), 0)),
            pl.BlockSpec((1, 2, GROUP, CHUNK, inner), lambda i: (0, 0, 0, at(i), 0)),
            pl.BlockSpec((CHUNK, inner), lambda i: (at(i), 0)),
            pl.BlockSpec((CHUNK, inner), lambda i: (at(i), 0)),
            whole(taps, 8, 128),
            pl.BlockSpec((2, CHUNK, inner), lambda i: (0, at(i), 0)),
            whole(*v2.shape),
            whole(*v1.shape),
        ],
        out_specs=pl.BlockSpec(
            (2, 1, tiles * GROUP, 128), lambda i: (0, jnp.maximum(i - chunks, 0), 0, 0)
        ),
        out_shape=jax.ShapeDtypeStruct((2, groups, tiles * GROUP, 128), f32),
        scratch_shapes=[
            pltpu.VMEM((rows, CHUNK, 2 * inner), f32),
            pltpu.VMEM((rows, 2, outer, inner), bf16),
        ],
        name="inverse",
    )(filtered, before, after, order(migration_shift), order(kernel_index), table, jnp.asarray(twist), jnp.asarray(v2), jnp.asarray(v1))
    return (
        image.reshape(2, groups, tiles, GROUP, 128)
        .transpose(0, 1, 3, 2, 4)
        .reshape(2, rows, pulses)
    )


def solution(mesh):
    return jax.shard_map(
        per_device,
        mesh=mesh,
        in_specs=(P(None, ("swath", "rng"), None), P(), P(), P(), P()),
        out_specs=P(None, ("swath", "rng"), None),
        check_vma=False,
    )
```

profile of v0, /device:TPU:17, one launch (start us, length us, event | category | flops | bytes accessed | tf_op | source)
XLA Modules:
  0.0 65.9 jit_solution(15202644546226154079)
XLA Ops:
  0.0 1.1 %multiply_bitcast_fusion = f32[1,2,256,128]{3,1,2,0:T(2,128)S(1)} fusion(f32[2,32768]{1,0:T(2,128)} %param.13), kind=kLoop, calls=%fused_computation.1 | loop fusion | flops 65536 | bytes 524288
  1.1 0.8 %copy.14 = f32[2,256,128]{1,2,0:T(8,128)} copy(f32[2,256,128]{2,1,0:T(8,128)S(1)} %bitcast.23) | data formatting | bytes 524288 | tf_op jit(solution)/shard_map/reshape | solution.py:161
  2.0 0.0 copy-start.3
  2.0 0.0 copy-start.1
  2.0 0.0 copy-start.2
  2.0 9.4 %forward.1.own_ref = bf16[2,2,8,128,256]{4,3,2,1,0:T(8,128)(2,1)} custom-call(f32[2,2,2048,128]{3,2,1,0:T(8,128)} %bitcast.21, bf16[256,256]{1,0:T(8,128)(2,1)} %constant.16.clone.w1h_ref, bf16[256,256]{1,0:T(8,128)(2,1)} %constant.17.clone.w1l_ref, bf16[512,512]{1,0:T(8,128)(2,1)} %constant.18.clone.w2h_ref, bf16[512,512]{1,0:T(8,128)(2,1)} %constant.19.clone.w2l_ref, ...), custom_call_target="tpu_custom_call" | custom-call | tf_op jit(solution)/shard_map/forward/pallas_call | solution.py:176
  11.4 3.7 %collective-permute-start = (bf16[2,2,8,128,256]{4,3,2,1,0:T(8,128)(2,1)}, bf16[2,2,8,128,256]{4,3,2,1,0:T(8,128)(2,1)S(1)}, u32[]{:S(2)}, u32[]{:S(2)}) collective-permute-start(bf16[2,2,8,128,256]{4,3,2,1,0:T(8,128)(2,1)} %forward.1.own_ref), channel_id=1, source_target_pairs={{0,1},{1,2},{2,3},{3,4},{4,5},{5,6},{6,7},{7,8},{8,9},{9,10},{10,1... | collective-permute-start | bytes 6291464 | tf_op jit(solution)/shard_map/ppermute | solution.py:193
  15.1 1.3 %slice.4 = bf16[1,2,8,128,256]{4,3,2,1,0:T(8,128)(2,1)S(1)} slice(bf16[2,2,8,128,256]{4,3,2,1,0:T(8,128)(2,1)} %forward.1.own_ref), slice={[0:1], [0:2], [0:8], [0:128], [0:256]} | slice | bytes 2097152 | tf_op jit(solution)/shard_map/slice | solution.py:194
  16.4 1.9 %collective-permute-start.1 = (bf16[1,2,8,128,256]{4,3,2,1,0:T(8,128)(2,1)S(1)}, bf16[1,2,8,128,256]{4,3,2,1,0:T(8,128)(2,1)}, u32[]{:S(2)}, u32[]{:S(2)}) collective-permute-start(bf16[1,2,8,128,256]{4,3,2,1,0:T(8,128)(2,1)S(1)} %slice.4), channel_id=1, source_target_pairs={{1,0},{2,1},{3,2},{4,3},{5,4},{6,5},{7,6},{8,7},{9,8},{10,9},{11,1... | collective-permute-start | bytes 3145736 | tf_op jit(solution)/shard_map/ppermute | solution.py:194
  18.3 0.0 copy-done.3
  18.3 0.1 copy.17
  18.4 0.1 tile.9
  18.5 0.0 copy-done.1
  18.5 0.7 %copy.15 = s32[256,128]{0,1:T(8,128)} copy(s32[256,128]{1,0:T(8,128)S(1)} %bitcast.26) | data formatting | bytes 262144 | tf_op jit(solution)/shard_map/reshape | solution.py:161
  19.3 0.0 copy-done.2
  19.3 0.8 %copy.16 = s32[256,128]{0,1:T(8,128)} copy(s32[256,128]{1,0:T(8,128)S(1)} %bitcast.27) | data formatting | bytes 262144 | tf_op jit(solution)/shard_map/reshape | solution.py:161
  20.0 31.2 %collective-permute-done.1.next_ref = bf16[1,2,8,128,256]{4,3,2,1,0:T(8,128)(2,1)} collective-permute-done((bf16[1,2,8,128,256]{4,3,2,1,0:T(8,128)(2,1)S(1)}, bf16[1,2,8,128,256]{4,3,2,1,0:T(8,128)(2,1)}, u32[]{:S(2)}, u32[]{:S(2)}) %collective-permute-start.1) | collective-permute-done | bytes 1048608 | tf_op jit(solution)/shard_map/ppermute | solution.py:194
  51.2 0.0 collective-permute-done.prev_ref
  51.2 0.0 copy-start
  51.2 0.7 %broadcast_in_dim.2.tab_ref = f32[16,8,128]{2,1,0:T(8,128)} broadcast(f32[16,128]{1,0:T(8,128)S(1)} %tile.9), dimensions={0,2} | broadcast | bytes 73728 | tf_op jit(solution)/shard_map/broadcast_in_dim | solution.py:195
  51.9 0.7 copy-done
  52.5 13.4 %inverse.1 = f32[2,2,2048,128]{3,2,1,0:T(8,128)} custom-call(bf16[2,2,8,128,256]{4,3,2,1,0:T(8,128)(2,1)} %forward.1.own_ref, bf16[2,2,8,128,256]{4,3,2,1,0:T(8,128)(2,1)} %copy-done, bf16[1,2,8,128,256]{4,3,2,1,0:T(8,128)(2,1)} %collective-permute-done.1.next_ref, s32[128,256]{1,0:T(8,128)} %bitcast.24, s32[128,256]{1,0:T(8,128)} %bitcast.25, ...), custom_call_target="tpu_custom_call" | custom-call | tf_op jit(solution)/shard_map/inverse/pallas_call | solution.py:201
  (2 shorter events, 0.0 us)
Async XLA Ops:
  2.0 16.4 %copy-start.3 = (f32[16,16]{1,0:T(8,128)S(1)}, f32[16,16]{1,0:T(8,128)}, u32[]{:S(2)}) copy-start(f32[16,16]{1,0:T(8,128)} %param.16) | copy-start | bytes 3076
  2.0 16.5 %copy-start.1 = (s32[32768]{0:T(1024)S(1)}, s32[32768]{0:T(1024)}, u32[]{:S(2)}) copy-start(s32[32768]{0:T(1024)} %param.14) | copy-start | bytes 393220
  2.0 17.3 %copy-start.2 = (s32[32768]{0:T(1024)S(1)}, s32[32768]{0:T(1024)}, u32[]{:S(2)}) copy-start(s32[32768]{0:T(1024)} %param.15) | copy-start | bytes 393220
  11.4 39.8 %collective-permute-start = (bf16[2,2,8,128,256]{4,3,2,1,0:T(8,128)(2,1)}, bf16[2,2,8,128,256]{4,3,2,1,0:T(8,128)(2,1)S(1)}, u32[]{:S(2)}, u32[]{:S(2)}) collective-permute-start(bf16[2,2,8,128,256]{4,3,2,1,0:T(8,128)(2,1)} %forward.1.own_ref), channel_id=1, source_target_pairs={{0,1},{1,2},{2,3},{3,4},{4,5},{5,6},{6,7},{7,8},{8,9},{9,10},{10,1... | collective-permute-start | bytes 6291464 | tf_op jit(solution)/shard_map/ppermute | solution.py:193
  16.4 34.8 %collective-permute-start.1 = (bf16[1,2,8,128,256]{4,3,2,1,0:T(8,128)(2,1)S(1)}, bf16[1,2,8,128,256]{4,3,2,1,0:T(8,128)(2,1)}, u32[]{:S(2)}, u32[]{:S(2)}) collective-permute-start(bf16[1,2,8,128,256]{4,3,2,1,0:T(8,128)(2,1)S(1)} %slice.4), channel_id=1, source_target_pairs={{1,0},{2,1},{3,2},{4,3},{5,4},{6,5},{7,6},{8,7},{9,8},{10,9},{11,1... | collective-permute-start | bytes 3145736 | tf_op jit(solution)/shard_map/ppermute | solution.py:194
  51.2 1.3 %copy-start = (bf16[2,2,8,128,256]{4,3,2,1,0:T(8,128)(2,1)}, bf16[2,2,8,128,256]{4,3,2,1,0:T(8,128)(2,1)S(1)}, u32[]{:S(2)}) copy-start(bf16[2,2,8,128,256]{4,3,2,1,0:T(8,128)(2,1)S(1)} %collective-permute-done.prev_ref) | copy-start | bytes 6291460
where the time goes:
time: 66.2 us; the launch traced here: 65.9 us
  waiting for transfers between devices  31.2 us (47%)
  Pallas kernels  22.8 us (34%)
  starting transfers between devices  5.61 us (8%)
  local copies, waits for them, and re-layouts  5.17 us (8%)
  other arithmetic  1.09 us (2%)
    ppermute x1, waiting for transfers between devices, per_device(): lax.ppermute(filtered[:1], 'rng', [(i + 1, i) for i in range(count - 1)])  31.2 us
    pallas_call x1, Pallas kernels, per_device(): pl.pallas_call(functools.partial(inverse_kernel, outer, inner, rows, taps...  13.4 us
    pallas_call x1, Pallas kernels, per_device(): pl.pallas_call(functools.partial(forward_kernel, outer, inner), grid=(gro...  9.44 us
    ppermute x1, starting transfers between devices, per_device(): lax.ppermute(filtered, 'rng', [(i, i + 1) for i in range(count - 1)])  3.69 us
    reshape x3, local copies, waits for them, and re-layouts, order(): table.reshape(table.shape[:-1] + (inner, outer))  2.34 us
    ppermute x1, starting transfers between devices, per_device(): lax.ppermute(filtered[:1], 'rng', [(i + 1, i) for i in range(count - 1)])  1.92 us
  transfers between devices with their start and end apart: 2, of which 1 were waited for; matrix products, arithmetic and copies ran while one was open for 5% of the time, Pallas kernels for 0%

commit v1 on v0

--- a/solution.py
+++ b/solution.py
@@ -88,6 +88,192 @@
             o_ref[0, 1, g * per + j] = (im * hr - re * hi).astype(bf16)
 
 
+def exchange_kernel(count, own, s_ref, prev, nxt, mid, low, head, mix, ssem, rsem, lsem):
+    me = lax.axis_index("rng")
+    role = me % 4
+    first = me < 4
+    final = me >= count - 4
+    half = own.shape[3] // 2
+    early, late = range(4), range(4, 8)
+
+    def at(ref, p):
+        group = (1 - p // 4) if ref.shape[0] == 2 else 0
+        return ref.at[group, (p // 2) % 2, :, pl.ds((p % 2) * half, half), :]
+
+    def copy(kind, p, src, dst, target):
+        return pltpu.make_async_remote_copy(
+            src_ref=at(src, p),
+            dst_ref=at(dst, p),
+            send_sem=ssem.at[kind, p],
+            recv_sem=rsem.at[kind, p],
+            device_id={"rng": target},
+            device_id_type=pl.DeviceIdType.MESH,
+        )
+
+    def got(kind, p, dst):
+        copy(kind, p, dst, dst, (me + 1) % count).wait_recv()
+
+    def merge(p, high, lower):
+        rows = pl.ds((p % 2) * half, half)
+        limit = SMAX - s_ref[rows, :]
+        for j in range(GROUP):
+            where = (0, (p // 2) % 2, j, rows)
+            mix[where] = jnp.where(
+                limit <= j, high[where].astype(f32), lower[where].astype(f32)
+            ).astype(bf16)
+
+    def local(src, dst, slot):
+        return pltpu.make_async_copy(src, dst, lsem.at[slot])
+
+    @pl.when(role == 0)
+    def _():
+        sends = [copy(0, p, own, prev, me + 1) for p in range(8)]
+        for s in sends:
+            s.start()
+
+        @pl.when(first)
+        def _():
+            low[...] = jnp.zeros_like(low)
+            fills = [local(low.at[0], prev.at[g], g) for g in range(2)]
+            for f in fills:
+                f.start()
+            for f in fills:
+                f.wait()
+
+        @pl.when(jnp.logical_not(first))
+        def _():
+            back = [copy(1, p, own, low, me - 3) for p in late]
+            for s in back:
+                s.start()
+            for p in range(8):
+                got(3, p, prev)
+            for s in back:
+                s.wait_send()
+
+        for p in late:
+            got(4, p, nxt)
+        for s in sends:
+            s.wait_send()
+
+    @pl.when(role == 1)
+    def _():
+        sends = [copy(2, p, own, prev, me + 1) for p in early]
+        sends += [copy(2, p, mix, prev, me + 1) for p in late]
+        back = [copy(4, p, own, nxt, me - 1) for p in late]
+        for p in early:
+            sends[p].start()
+        for s in back:
+            s.start()
+        fetch = local(own.at[0], head.at[0], 0)
+        fetch.start()
+        fetch.wait()
+
+        @pl.when(final)
+        def _():
+            low[...] = jnp.zeros_like(low)
+
+        def relay(p):
+            got(2, p, mid)
+
+            @pl.when(jnp.logical_not(final))
+            def _():
+                copy(3, p, mid, prev, me + 3).start()
+
+        for p in early:
+
+            @pl.when(jnp.logical_not(final))
+            def _():
+                got(1, p + 4, low)
+
+            merge(p + 4, head, low)
+            sends[p + 4].start()
+            relay(p)
+        for p in late:
+            relay(p)
+        out = local(mid.at[0], nxt.at[0], 1)
+        out.start()
+        for p in range(8):
+            got(0, p, prev)
+        out.wait()
+        for s in sends + back:
+            s.wait_send()
+
+        @pl.when(jnp.logical_not(final))
+        def _():
+            for p in range(8):
+                copy(3, p, mid, prev, me + 3).wait_send()
+
+    @pl.when(role == 2)
+    def _():
+        fetch = local(own.at[0], head.at[0], 0)
+        fetch.start()
+        sends = [copy(0, p, own, prev, me + 1) for p in range(8)]
+        for s in sends:
+            s.start()
+        over = [copy(2, p, mid, mid, me - 1) for p in early]
+        over += [copy(2, p, mix, mid, me - 1) for p in late]
+        for p in early:
+            got(0, p, mid)
+            over[p].start()
+        fetch.wait()
+        for p in late:
+            got(0, p, mid)
+            merge(p, mid, head)
+            over[p].start()
+        out = local(mid.at[0], nxt.at[0], 1)
+        out.start()
+        pass_on = [copy(3, p, prev, nxt, me + 1) for p in late]
+        for p in early:
+            got(2, p, prev)
+        for p in late:
+            got(2, p, prev)
+            pass_on[p - 4].start()
+        out.wait()
+        for s in sends + over + pass_on:
+            s.wait_send()
+
+    @pl.when(role == 3)
+    def _():
+        sends = [copy(0, p, own, mid, me - 1) for p in range(8)]
+        for s in sends:
+            s.start()
+        for p in range(8):
+            got(0, p, prev)
+        for p in late:
+            got(3, p, nxt)
+        for s in sends:
+            s.wait_send()
+
+
+def exchange(filtered, shift, count):
+    if count % 4 or filtered.shape[0] != 2 or filtered.shape[2] != SMAX - 1:
+        before = lax.ppermute(filtered, "rng", [(i, i + 1) for i in range(count - 1)])
+        after = lax.ppermute(filtered[:1], "rng", [(i + 1, i) for i in range(count - 1)])
+        return before, after
+    short = (1,) + filtered.shape[1:]
+    anywhere = pl.BlockSpec(memory_space=pl.ANY)
+    return pl.pallas_call(
+        functools.partial(exchange_kernel, count),
+        in_specs=[anywhere, pl.BlockSpec(memory_space=pltpu.VMEM)],
+        out_specs=[anywhere, anywhere],
+        out_shape=[
+            jax.ShapeDtypeStruct(filtered.shape, bf16),
+            jax.ShapeDtypeStruct(short, bf16),
+        ],
+        scratch_shapes=[
+            pltpu.VMEM(filtered.shape, bf16),
+            pltpu.VMEM(short, bf16),
+            pltpu.VMEM(short, bf16),
+            pltpu.VMEM(short, bf16),
+            pltpu.SemaphoreType.DMA((5, 8)),
+            pltpu.SemaphoreType.DMA((5, 8)),
+            pltpu.SemaphoreType.DMA((2,)),
+        ],
+        compiler_params=pltpu.CompilerParams(has_side_effects=True),
+        name="exchange",
+    )(filtered, shift)
+
+
 def inverse_kernel(outer, inner, rows, taps, chunks, own_ref, prev_ref, next_ref, s_ref, k_ref, tab_ref, t_ref, v2_ref, v1_ref, o_ref, m_ref, y_ref):
     lanes = 128
     parts = inner // lanes
@@ -190,8 +376,8 @@
         scratch_shapes=[pltpu.VMEM((GROUP * outer, 2 * inner), bf16)] * 2,
         name="forward",
     )(signal, jnp.asarray(w1h), jnp.asarray(w1l), jnp.asarray(w2h), jnp.asarray(w2l), jnp.asarray(twist), response)
-    before = lax.ppermute(filtered, "rng", [(i, i + 1) for i in range(count - 1)])
-    after = lax.ppermute(filtered[:1], "rng", [(i + 1, i) for i in range(count - 1)])
+    shift = order(migration_shift)
+    before, after = exchange(filtered, shift, count)
     table = jnp.broadcast_to(
         jnp.tile(kernel_taps.T, (1, 128 // kernel_taps.shape[0]))[:, None, :], (taps, 8, 128)
     )
@@ -221,7 +407,7 @@
             pltpu.VMEM((rows, 2, outer, inner), bf16),
         ],
         name="inverse",
-    )(filtered, before, after, order(migration_shift), order(kernel_index), table, jnp.asarray(twist), jnp.asarray(v2), jnp.asarray(v1))
+    )(filtered, before, after, shift, order(kernel_index), table, jnp.asarray(twist), jnp.asarray(v2), jnp.asarray(v1))
     return (
         image.reshape(2, groups, tiles, GROUP, 128)
         .transpose(0, 1, 3, 2, 4)

time: 66.2 us -> 68.8 us (1.039)
  the two profiles are of different devices: /device:TPU:17 before, /device:TPU:8 now
where the time goes in v1:
time: 68.8 us; the launch traced here: 68.2 us
  Pallas kernels  61.4 us (89%)
  local copies, waits for them, and re-layouts  5.67 us (8%)
  other arithmetic  1.09 us (2%)
    pallas_call x1, Pallas kernels, exchange(): pl.pallas_call(functools.partial(exchange_kernel, count), in_specs=[anywh...  38.6 us
    pallas_call x1, Pallas kernels, per_device(): pl.pallas_call(functools.partial(inverse_kernel, outer, inner, rows, taps...  13.4 us
    pallas_call x1, Pallas kernels, per_device(): pl.pallas_call(functools.partial(forward_kernel, outer, inner), grid=(gro...  9.37 us
    reshape x3, local copies, waits for them, and re-layouts, order(): table.reshape(table.shape[:-1] + (inner, outer))  4.16 us

profile of v1, /device:TPU:8, one launch (start us, length us, event | category | flops | bytes accessed | tf_op | source)
XLA Modules:
  0.0 68.2 jit_solution(16246006356055656220)
XLA Ops:
  0.0 0.8 %copy.17 = f32[16,16]{1,0:T(8,128)S(1)} copy(f32[16,16]{0,1:T(8,128)} %bitcast.29) | data formatting | bytes 2048 | tf_op jit(solution)/shard_map/transpose | solution.py:382
  0.8 0.1 tile.9
  0.9 0.6 broadcast_in_dim.2.tab_ref
  1.5 1.7 %copy.15 = s32[256,128]{0,1:T(8,128)} copy(s32[256,128]{1,0:T(8,128)} %bitcast.27) | data formatting | bytes 262144 | tf_op jit(solution)/shard_map/reshape | solution.py:347
  3.1 1.7 %copy.16 = s32[256,128]{0,1:T(8,128)} copy(s32[256,128]{1,0:T(8,128)} %bitcast.28) | data formatting | bytes 262144 | tf_op jit(solution)/shard_map/reshape | solution.py:347
  4.8 1.1 %multiply_bitcast_fusion = f32[1,2,256,128]{3,1,2,0:T(2,128)S(1)} fusion(f32[2,32768]{1,0:T(2,128)} %param.13), kind=kLoop, calls=%fused_computation.1 | loop fusion | flops 65536 | bytes 524288
  5.9 0.8 %copy.14 = f32[2,256,128]{1,2,0:T(8,128)} copy(f32[2,256,128]{2,1,0:T(8,128)S(1)} %bitcast.25) | data formatting | bytes 524288 | tf_op jit(solution)/shard_map/reshape | solution.py:347
  6.8 9.4 %forward.1.own.own_ref = bf16[2,2,8,128,256]{4,3,2,1,0:T(8,128)(2,1)} custom-call(f32[2,2,2048,128]{3,2,1,0:T(8,128)} %bitcast.21, bf16[256,256]{1,0:T(8,128)(2,1)} %constant.16.clone.w1h_ref, bf16[256,256]{1,0:T(8,128)(2,1)} %constant.17.clone.w1l_ref, bf16[512,512]{1,0:T(8,128)(2,1)} %constant.18.clone.w2h_ref, bf16[512,512]{1,0:T(8,128)(2,1)} %constant.19.clone.w2l_ref, ...), custom_call_target="tpu_custom_call" | custom-call | tf_op jit(solution)/shard_map/forward/pallas_call | solution.py:362
  16.1 38.6 %exchange.1 = (bf16[2,2,8,128,256]{4,3,2,1,0:T(8,128)(2,1)}, bf16[1,2,8,128,256]{4,3,2,1,0:T(8,128)(2,1)}) custom-call(bf16[2,2,8,128,256]{4,3,2,1,0:T(8,128)(2,1)} %forward.1.own.own_ref, s32[128,256]{1,0:T(8,128)} %bitcast.22), custom_call_target="tpu_custom_call" | custom-call | tf_op jit(solution)/shard_map/exchange/pallas_call | solution.py:255
  54.7 13.4 %inverse.1 = f32[2,2,2048,128]{3,2,1,0:T(8,128)} custom-call(bf16[2,2,8,128,256]{4,3,2,1,0:T(8,128)(2,1)} %forward.1.own.own_ref, bf16[2,2,8,128,256]{4,3,2,1,0:T(8,128)(2,1)} %get-tuple-element.7.prev_ref, bf16[1,2,8,128,256]{4,3,2,1,0:T(8,128)(2,1)} %get-tuple-element.8.next_ref, s32[128,256]{1,0:T(8,128)} %bitcast.23, s32[128,256]{1,0:T(8,128)} %bitcast.26, ...), custom_call_target="tpu_custom_call" | custom-call | tf_op jit(solution)/shard_map/inverse/pallas_call | solution.py:387
  (2 shorter events, 0.0 us)

commit v2 on v1

--- a/solution.py
+++ b/solution.py
@@ -46,10 +46,14 @@
     return high, (value - high.astype(f32)).astype(bf16)
 
 
-def forward_kernel(outer, inner, x_ref, w1h_ref, w1l_ref, w2h_ref, w2l_ref, t_ref, h_ref, o_ref, rh_ref, rl_ref):
+def forward_kernel(outer, inner, x_ref, w1h_ref, w1l_ref, w2h_ref, w2l_ref, t_ref, h_ref, s_ref, k_ref, o_ref, so_ref, ko_ref, rh_ref, rl_ref):
     lanes = 128
     parts = inner // lanes
     stride = GROUP * parts
+    so_ref[...] = s_ref[...].T
+    ko_ref[...] = k_ref[...].T
+    norm = 1.0 / math.sqrt(outer * inner)
+    hr, hi = h_ref[0].T * norm, h_ref[1].T * norm
     w1h = w1h_ref[...]
     w1l = w1l_ref[...]
     for r in range(GROUP):
@@ -83,7 +87,6 @@
         for j in range(per):
             re = z[j * outer : (j + 1) * outer, :inner]
             im = z[j * outer : (j + 1) * outer, inner:]
-            hr, hi = h_ref[0], h_ref[1]
             o_ref[0, 0, g * per + j] = (re * hr + im * hi).astype(bf16)
             o_ref[0, 1, g * per + j] = (im * hr - re * hi).astype(bf16)
 
@@ -145,7 +148,9 @@
             back = [copy(1, p, own, low, me - 3) for p in late]
             for s in back:
                 s.start()
-            for p in range(8):
+            for p in early:
+                got(2, p, prev)
+            for p in late:
                 got(3, p, prev)
             for s in back:
                 s.wait_send()
@@ -179,17 +184,15 @@
             def _():
                 copy(3, p, mid, prev, me + 3).start()
 
-        for p in early:
+        for p in late:
+            relay(p)
 
             @pl.when(jnp.logical_not(final))
             def _():
-                got(1, p + 4, low)
-
-            merge(p + 4, head, low)
-            sends[p + 4].start()
-            relay(p)
-        for p in late:
-            relay(p)
+                got(1, p, low)
+
+            merge(p, head, low)
+            sends[p].start()
         out = local(mid.at[0], nxt.at[0], 1)
         out.start()
         for p in range(8):
@@ -200,7 +203,7 @@
 
         @pl.when(jnp.logical_not(final))
         def _():
-            for p in range(8):
+            for p in late:
                 copy(3, p, mid, prev, me + 3).wait_send()
 
     @pl.when(role == 2)
@@ -210,19 +213,22 @@
         sends = [copy(0, p, own, prev, me + 1) for p in range(8)]
         for s in sends:
             s.start()
-        over = [copy(2, p, mid, mid, me - 1) for p in early]
-        over += [copy(2, p, mix, mid, me - 1) for p in late]
-        for p in early:
-            got(0, p, mid)
-            over[p].start()
+        over = [copy(2, p, mix, mid, me - 1) for p in late]
         fetch.wait()
         for p in late:
             got(0, p, mid)
             merge(p, mid, head)
-            over[p].start()
+            over[p - 4].start()
         out = local(mid.at[0], nxt.at[0], 1)
         out.start()
         pass_on = [copy(3, p, prev, nxt, me + 1) for p in late]
+
+        @pl.when(jnp.logical_not(first))
+        def _():
+            for p in early:
+                got(3, p, mid)
+                copy(2, p, mid, prev, me - 2).start()
+
         for p in early:
             got(2, p, prev)
         for p in late:
@@ -232,17 +238,33 @@
         for s in sends + over + pass_on:
             s.wait_send()
 
+        @pl.when(jnp.logical_not(first))
+        def _():
+            for p in early:
+                copy(2, p, mid, prev, me - 2).wait_send()
+
     @pl.when(role == 3)
     def _():
-        sends = [copy(0, p, own, mid, me - 1) for p in range(8)]
+        sends = [copy(0, p, own, mid, me - 1) for p in late]
         for s in sends:
             s.start()
+
+        @pl.when(jnp.logical_not(final))
+        def _():
+            for p in early:
+                copy(3, p, own, mid, me + 3).start()
+
         for p in range(8):
             got(0, p, prev)
         for p in late:
             got(3, p, nxt)
         for s in sends:
             s.wait_send()
+
+        @pl.when(jnp.logical_not(final))
+        def _():
+            for p in early:
+                copy(3, p, own, mid, me + 3).wait_send()
 
 
 def exchange(filtered, shift, count):
@@ -343,9 +365,6 @@
     count = lax.axis_size("rng")
     whole = lambda *shape: pl.BlockSpec(shape, lambda i: (0,) * len(shape))
 
-    def order(table):
-        return jnp.swapaxes(table.reshape(table.shape[:-1] + (inner, outer)), -1, -2)
-
     oc, osn = dft(outer)
     ic, isn = dft(inner)
     w1h, w1l = split(np.block([[oc, osn], [-osn, oc]]))
@@ -353,13 +372,12 @@
     v2 = split(np.block([[ic, isn], [-isn, ic]]))[0]
     v1 = split(np.block([[oc, -osn], [osn, oc]]))[0]
     twist = twiddles(outer, inner)
-    response = order(doppler_filter * (1.0 / math.sqrt(pulses)))
     signal = (
         echoes.reshape(2, groups, GROUP, tiles, 128)
         .transpose(0, 1, 3, 2, 4)
         .reshape(2, groups, tiles * GROUP, 128)
     )
-    filtered = pl.pallas_call(
+    filtered, shift, which = pl.pallas_call(
         functools.partial(forward_kernel, outer, inner),
         grid=(groups,),
         in_specs=[
@@ -369,14 +387,23 @@
             whole(*w2h.shape),
             whole(*w2h.shape),
             whole(*twist.shape),
-            whole(*twist.shape),
-        ],
-        out_specs=pl.BlockSpec((1, 2, GROUP, outer, inner), lambda i: (i, 0, 0, 0, 0)),
-        out_shape=jax.ShapeDtypeStruct((groups, 2, GROUP, outer, inner), bf16),
+            whole(2, inner, outer),
+            whole(inner, outer),
+            whole(inner, outer),
+        ],
+        out_specs=[
+            pl.BlockSpec((1, 2, GROUP, outer, inner), lambda i: (i, 0, 0, 0, 0)),
+            whole(outer, inner),
+            whole(outer, inner),
+        ],
+        out_shape=[
+            jax.ShapeDtypeStruct((groups, 2, GROUP, outer, inner), bf16),
+            jax.ShapeDtypeStruct((outer, inner), jnp.int32),
+            jax.ShapeDtypeStruct((outer, inner), jnp.int32),
+        ],
         scratch_shapes=[pltpu.VMEM((GROUP * outer, 2 * inner), bf16)] * 2,
         name="forward",
-    )(signal, jnp.asarray(w1h), jnp.asarray(w1l), jnp.asarray(w2h), jnp.asarray(w2l), jnp.asarray(twist), response)
-    shift = order(migration_shift)
+    )(signal, jnp.asarray(w1h), jnp.asarray(w1l), jnp.asarray(w2h), jnp.asarray(w2l), jnp.asarray(twist), doppler_filter.reshape(2, inner, outer), migration_shift.reshape(inner, outer), kernel_index.reshape(inner, outer))
     before, after = exchange(filtered, shift, count)
     table = jnp.broadcast_to(
         jnp.tile(kernel_taps.T, (1, 128 // kernel_taps.shape[0]))[:, None, :], (taps, 8, 128)
@@ -407,7 +434,7 @@
             pltpu.VMEM((rows, 2, outer, inner), bf16),
         ],
         name="inverse",
-    )(filtered, before, after, shift, order(kernel_index), table, jnp.asarray(twist), jnp.asarray(v2), jnp.asarray(v1))
+    )(filtered, before, after, shift, which, table, jnp.asarray(twist), jnp.asarray(v2), jnp.asarray(v1))
     return (
         image.reshape(2, groups, tiles, GROUP, 128)
         .transpose(0, 1, 3, 2, 4)

time: 68.8 us -> 61.2 us (0.89)
  Pallas kernels: 61.4 us -> 57.7 us
  local copies, waits for them, and re-layouts: 5.67 us -> 3.17 us
  other arithmetic: 1.09 us -> 0 us
    reshape x3 -> x0, local copies, waits for them, and re-layouts: 4.16 us -> none  [order(): table.reshape(table.shape[:-1] + (inner, outer))]
    pallas_call x1, Pallas kernels: 38.6 us -> 34.6 us  [exchange(): pl.pallas_call(functools.partial(exchange_kernel, count), in_specs=[anywh...]
    unnamed x1, local copies, waits for them, and re-layouts: 0.02 us -> 1.67 us
    unnamed x1 -> x0, other arithmetic: 1.09 us -> none
where the time goes in v2:
time: 61.2 us; the launch traced here: 60.9 us
  Pallas kernels  57.7 us (94%)
  local copies, waits for them, and re-layouts  3.17 us (5%)
    pallas_call x1, Pallas kernels, exchange(): pl.pallas_call(functools.partial(exchange_kernel, count), in_specs=[anywh...  34.6 us
    pallas_call x1, Pallas kernels, per_device(): pl.pallas_call(functools.partial(inverse_kernel, outer, inner, rows, taps...  13.4 us
    pallas_call x1, Pallas kernels, per_device(): pl.pallas_call(functools.partial(forward_kernel, outer, inner), grid=(gro...  9.66 us
    unnamed x1, local copies, waits for them, and re-layouts  1.67 us

profile of v2, /device:TPU:8, one launch (start us, length us, event | category | flops | bytes accessed | tf_op | source)
XLA Modules:
  0.0 60.9 jit_solution(15607094312490157503)
XLA Ops:
  0.0 0.8 %copy.13 = f32[16,16]{1,0:T(8,128)S(1)} copy(f32[16,16]{0,1:T(8,128)} %bitcast.22) | data formatting | bytes 2048 | tf_op jit(solution)/shard_map/transpose | solution.py:409
  0.8 0.1 tile.9
  0.9 0.6 %broadcast_in_dim.2.tab_ref = f32[16,8,128]{2,1,0:T(8,128)} broadcast(f32[16,128]{1,0:T(8,128)S(1)} %tile.9), dimensions={0,2} | broadcast | bytes 73728 | tf_op jit(solution)/shard_map/broadcast_in_dim | solution.py:408
  1.5 1.7 %copy.16 = f32[1,2,256,128]{3,2,1,0:T(8,128)} copy(f32[1,2,256,128]{3,1,2,0:T(2,128)} %bitcast.19) | data formatting | bytes 524288
  3.2 9.7 %forward.1 = (bf16[2,2,8,128,256]{4,3,2,1,0:T(8,128)(2,1)}, s32[128,256]{1,0:T(8,128)}, s32[128,256]{1,0:T(8,128)}) custom-call(f32[2,2,2048,128]{3,2,1,0:T(8,128)} %bitcast.17, bf16[256,256]{1,0:T(8,128)(2,1)} %constant.14.clone.w1h_ref, bf16[256,256]{1,0:T(8,128)(2,1)} %constant.15.clone.w1l_ref, bf16[512,512]{1,0:T(8,128)(2,1)} %constant.16.clone.w2h_ref, ...), custom_call_target="tpu_custom_call" | custom-call | tf_op jit(solution)/shard_map/forward/pallas_call | solution.py:380
  12.8 34.6 %exchange.1 = (bf16[2,2,8,128,256]{4,3,2,1,0:T(8,128)(2,1)}, bf16[1,2,8,128,256]{4,3,2,1,0:T(8,128)(2,1)}) custom-call(bf16[2,2,8,128,256]{4,3,2,1,0:T(8,128)(2,1)} %get-tuple-element.10.own.own_ref, s32[128,256]{1,0:T(8,128)} %get-tuple-element.11.s_ref), custom_call_target="tpu_custom_call" | custom-call | tf_op jit(solution)/shard_map/exchange/pallas_call | solution.py:277
  47.5 13.4 %inverse.1 = f32[2,2,2048,128]{3,2,1,0:T(8,128)} custom-call(bf16[2,2,8,128,256]{4,3,2,1,0:T(8,128)(2,1)} %get-tuple-element.10.own.own_ref, bf16[2,2,8,128,256]{4,3,2,1,0:T(8,128)(2,1)} %get-tuple-element.12.prev_ref, bf16[1,2,8,128,256]{4,3,2,1,0:T(8,128)(2,1)} %get-tuple-element.13.next_ref, s32[128,256]{1,0:T(8,128)} %get-tuple-element.11.s_ref, ...), custom_call_target="tpu_custom_call" | custom-call | tf_op jit(solution)/shard_map/inverse/pallas_call | solution.py:414
  (1 shorter events, 0.0 us)

commit v3 on v2

--- a/solution.py
+++ b/solution.py
@@ -313,7 +313,7 @@
                 which = k_ref[a, b]
                 bits = [(offset & bit) != 0 for bit in (8, 4, 2, 1)]
                 weights = [
-                    jnp.take_along_axis(tab_ref[k], which, axis=1, mode="promise_in_bounds")
+                    jnp.take_along_axis(jnp.broadcast_to(tab_ref[k : k + 1, :], (8, 128)), which, axis=1, mode="promise_in_bounds")
                     for k in range(taps)
                 ]
                 for c in range(2):
@@ -405,9 +405,7 @@
         name="forward",
     )(signal, jnp.asarray(w1h), jnp.asarray(w1l), jnp.asarray(w2h), jnp.asarray(w2l), jnp.asarray(twist), doppler_filter.reshape(2, inner, outer), migration_shift.reshape(inner, outer), kernel_index.reshape(inner, outer))
     before, after = exchange(filtered, shift, count)
-    table = jnp.broadcast_to(
-        jnp.tile(kernel_taps.T, (1, 128 // kernel_taps.shape[0]))[:, None, :], (taps, 8, 128)
-    )
+    table = jnp.pad(kernel_taps.T, ((0, 0), (0, 128 - kernel_taps.shape[0])))
     chunks = outer // CHUNK
     last = chunks - 1
     at = lambda i: jnp.minimum(i, last)
@@ -420,7 +418,7 @@
             pl.BlockSpec((1, 2, GROUP, CHUNK, inner), lambda i: (0, 0, 0, at(i), 0)),
             pl.BlockSpec((CHUNK, inner), lambda i: (at(i), 0)),
             pl.BlockSpec((CHUNK, inner), lambda i: (at(i), 0)),
-            whole(taps, 8, 128),
+            whole(taps, 128),
             pl.BlockSpec((2, CHUNK, inner), lambda i: (0, at(i), 0)),
             whole(*v2.shape),
             whole(*v1.shape),

time: 61.2 us -> 61.1 us (level)
    unnamed x1 -> x2, local copies, waits for them, and re-layouts: 1.67 us -> 2.43 us
    transpose x1 -> x0, local copies, waits for them, and re-layouts: 0.77 us -> none  [per_device(): table = jnp.broadcast_to(jnp.tile(kernel_taps.T, (1, 128 // kernel_taps.s...]
    broadcast_in_dim x1 -> x0, local copies, waits for them, and re-layouts: 0.65 us -> none  [per_device(): jnp.broadcast_to(jnp.tile(kernel_taps.T, (1, 128 // kernel_taps.shape[0])...]
where the time goes in v3:
time: 61.1 us; the launch traced here: 60.8 us
  Pallas kernels  57.8 us (95%)
  local copies, waits for them, and re-layouts  3.03 us (5%)
    pallas_call x1, Pallas kernels, exchange(): pl.pallas_call(functools.partial(exchange_kernel, count), in_specs=[anywh...  34.6 us
    pallas_call x1, Pallas kernels, per_device(): pl.pallas_call(functools.partial(inverse_kernel, outer, inner, rows, taps...  13.5 us
    pallas_call x1, Pallas kernels, per_device(): pl.pallas_call(functools.partial(forward_kernel, outer, inner), grid=(gro...  9.68 us
    unnamed x2, local copies, waits for them, and re-layouts  2.43 us

profile of v3, /device:TPU:8, one launch (start us, length us, event | category | flops | bytes accessed | tf_op | source)
XLA Modules:
  0.0 60.8 jit_solution(18373403707127772550)
XLA Ops:
  0.0 0.8 %copy.13 = f32[16,16]{0,1:T(8,128)S(1)} copy(f32[16,16]{1,0:T(8,128)} %param.16) | data formatting | bytes 2048 | tf_op args[4]
  0.8 0.6 pad.4.tab_ref
  1.4 1.7 %copy.16 = f32[1,2,256,128]{3,2,1,0:T(8,128)} copy(f32[1,2,256,128]{3,1,2,0:T(2,128)} %bitcast.19) | data formatting | bytes 524288
  3.0 9.7 %forward.1 = (bf16[2,2,8,128,256]{4,3,2,1,0:T(8,128)(2,1)}, s32[128,256]{1,0:T(8,128)}, s32[128,256]{1,0:T(8,128)}) custom-call(f32[2,2,2048,128]{3,2,1,0:T(8,128)} %bitcast.17, bf16[256,256]{1,0:T(8,128)(2,1)} %constant.17.clone.w1h_ref, bf16[256,256]{1,0:T(8,128)(2,1)} %constant.18.clone.w1l_ref, bf16[512,512]{1,0:T(8,128)(2,1)} %constant.19.clone.w2h_ref, ...), custom_call_target="tpu_custom_call" | custom-call | tf_op jit(solution)/shard_map/forward/pallas_call | solution.py:380
  12.7 34.6 %exchange.1 = (bf16[2,2,8,128,256]{4,3,2,1,0:T(8,128)(2,1)}, bf16[1,2,8,128,256]{4,3,2,1,0:T(8,128)(2,1)}) custom-call(bf16[2,2,8,128,256]{4,3,2,1,0:T(8,128)(2,1)} %get-tuple-element.10.own.own_ref, s32[128,256]{1,0:T(8,128)} %get-tuple-element.11.s_ref), custom_call_target="tpu_custom_call" | custom-call | tf_op jit(solution)/shard_map/exchange/pallas_call | solution.py:277
  47.3 13.5 %inverse.1 = f32[2,2,2048,128]{3,2,1,0:T(8,128)} custom-call(bf16[2,2,8,128,256]{4,3,2,1,0:T(8,128)(2,1)} %get-tuple-element.10.own.own_ref, bf16[2,2,8,128,256]{4,3,2,1,0:T(8,128)(2,1)} %get-tuple-element.12.prev_ref, bf16[1,2,8,128,256]{4,3,2,1,0:T(8,128)(2,1)} %get-tuple-element.13.next_ref, s32[128,256]{1,0:T(8,128)} %get-tuple-element.11.s_ref, ...), custom_call_target="tpu_custom_call" | custom-call | tf_op jit(solution)/shard_map/inverse/pallas_call | solution.py:412
